TPU v7x, 32 devices: a whole 2x2x4 slice. The times are simulated.
32 devices in a mesh: groups: 2 (over y), dp: 4 (over x, core), mp: 4 (over z).
Axes of the slice: x: 2, y: 2, z: 4, core: 2. Of those that a mesh axis runs over, the one named last changes fastest.
Arguments:
- base_states: bfloat16 [1280, 4096], P(('groups', 'dp'), 'mp'), parts along dimension 0, may hold values from -6 to 6
- source_states: bfloat16 [1280, 4096], P(('groups', 'dp'), 'mp'), parts along dimension 0, may hold values from -6 to 6
- source_rank: int32 [1280, 1], P(('groups', 'dp')), parts along dimension 0, may hold values from 0 to 3; in each aligned block of 160 rows (0 to 159, 160 to 319, ...) at most 80 rows name the same one
- source_row: int32 [1280], P(('groups', 'dp')), parts along dimension 0, may hold values from 0 to 159
- rotation: bfloat16 [4096, 4096], P(None, 'mp'), may hold values from -0.125 to 0.125
- mask_logits: float32 [4096], P('mp'), may hold values from -8 to 8
- norm_gain: bfloat16 [4096], replicated, may hold values from 0.25 to 1.75
- gate_weight: bfloat16 [4096, 14336], P(None, 'mp'), may hold values from -0.09375 to 0.09375
- up_weight: bfloat16 [4096, 14336], P(None, 'mp'), may hold values from -0.09375 to 0.09375
- hidden_cot: bfloat16 [1280, 14336], P(('groups', 'dp'), 'mp'), parts along dimension 0, may hold values from -0.23632812 to 0.23632812
Outputs:
- rotation_grad: float32 [8192, 4096], P(('groups', 'dp'), 'mp'), parts along dimension 0
- interchanged: bfloat16 [1280, 4096], P(('groups', 'dp'), 'mp'), parts along dimension 0
There are 2 independent parts, one for each index of `groups`. A program takes and returns all parts, laid end to end along the dimension named above; an argument that names none is the same for every part. Nothing has to cross between parts.
Inputs may be any that keep to these rules, and one draw needn't show every extreme that they name: `source_rank`: within the 160 tokens of each dp index, no dp index is named more than 80 times, and some dp index is named exactly 80 times by the tokens of some dp index.
All inputs are finite; a program needn't handle non-finite values.
Results may differ from a plain program's by a relative error of at most 0.014.
Values may be sent and summed in bfloat16 or wider, within the bound.
A program may use at most 192 MiB of HBM per device.

v0:
```python
import jax
import jax.numpy as jnp
from jax import lax
from jax.sharding import PartitionSpec as P


def contract_first(left, right):
    return lax.dot_general(
        left, right, (((0,), (0,)), ((), ())), preferred_element_type=jnp.float32
    )


def contract_last(left, right):
    return lax.dot_general(
        left, right, (((1,), (1,)), ((), ())), preferred_element_type=jnp.float32
    )


def shards(
    base_states,
    source_states,
    source_rank,
    source_row,
    rotation,
    mask_logits,
    norm_gain,
    gate_weight,
    up_weight,
    hidden_cot,
):
    tokens = base_states.shape[0]
    width = rotation.shape[0]
    ranks_of = source_rank[:, 0]
    everyone = lax.all_gather(source_states, "dp", axis=0, tiled=True)
    paired = jnp.take(everyone, ranks_of * tokens + source_row, axis=0)
    diff_local = (paired.astype(jnp.float32) - base_states.astype(jnp.float32)).astype(jnp.bfloat16)
    diff_full = lax.all_gather(diff_local, "mp", axis=1, tiled=True)
    mask = jax.nn.sigmoid(mask_logits)[None, :]
    coords = jnp.dot(diff_full, rotation, preferred_element_type=jnp.float32)
    weighted = (mask * coords).astype(jnp.bfloat16)
    moved = lax.psum_scatter(
        contract_last(rotation, weighted), "mp", scatter_dimension=0, tiled=True
    ).T
    interchanged = (base_states.astype(jnp.float32) + moved).astype(jnp.bfloat16)
    full_rows = lax.all_gather(interchanged, "mp", axis=1, tiled=True)
    states = full_rows.astype(jnp.float32)
    gain_f = norm_gain.astype(jnp.float32)[None, :]
    recip = lax.rsqrt(jnp.mean(states * states, axis=1, keepdims=True) + 1e-05)
    normed = (states * recip * gain_f).astype(jnp.bfloat16)
    gate = jnp.dot(normed, gate_weight, preferred_element_type=jnp.float32)
    up_val = jnp.dot(normed, up_weight, preferred_element_type=jnp.float32)
    sigm = jax.nn.sigmoid(gate)
    cotan = hidden_cot.astype(jnp.float32)
    dgate = (cotan * up_val * sigm * (1.0 + gate * (1.0 - sigm))).astype(jnp.bfloat16)
    dup_val = (cotan * gate * sigm).astype(jnp.bfloat16)
    partial_grad = contract_last(dgate, gate_weight) + contract_last(dup_val, up_weight)
    dnormed = lax.psum(partial_grad, "mp")
    scaled = gain_f * dnormed
    stat = jnp.sum(scaled * states, axis=1, keepdims=True)
    dinter = (recip * scaled - states * recip * recip * recip * stat / width).astype(jnp.bfloat16)
    coupled = (mask * jnp.dot(dinter, rotation, preferred_element_type=jnp.float32)).astype(
        jnp.bfloat16
    )
    rotation_grad = lax.psum_scatter(
        (contract_first(dinter, weighted) + contract_first(diff_full, coupled)).astype(
            jnp.bfloat16
        ),
        "dp",
        scatter_dimension=0,
        tiled=True,
    ).astype(jnp.float32)
    return (rotation_grad, interchanged)


def solution(mesh):
    placed = (
        P(("groups", "dp"), "mp"),
        P(("groups", "dp"), "mp"),
        P(("groups", "dp"), None),
        P(("groups", "dp")),
        P(None, "mp"),
        P("mp"),
        P(),
        P(None, "mp"),
        P(None, "mp"),
        P(("groups", "dp"), "mp"),
    )
    return jax.shard_map(
        shards,
        mesh=mesh,
        in_specs=placed,
        out_specs=(P(("groups", "dp"), "mp"), P(("groups", "dp"), "mp")),
        check_vma=False,
    )
```

profile of v0, /device:TPU:0, one launch (start us, length us, event | category | flops | bytes accessed | tf_op | source)
XLA Modules:
  0.0 437.6 jit_solution(6503187175433024214)
XLA Ops:
  7.2 0.0 all-gather.4.cloned.1.call-start
  7.2 0.7 all-gather.4.cloned.1.call-update
  7.9 0.0 all-gather.6.cloned.1.call-start
  8.0 0.7 broadcast_multiply_fusion
  8.6 0.7 compare_and_fusion
  9.3 21.2 %all-gather.4.cloned.1.call-done = bf16[640,1024]{1,0:T(8,128)(2,1)} async-done(((bf16[160,1024]{1,0:T(8,128)(2,1)}), bf16[640,1024]{1,0:T(8,128)(2,1)}) %all-gather.4.cloned.1.call-update) | async-done | bytes 1310736 | tf_op jit(solution)/shard_map/all_gather | solution.py:34
  30.5 2.7 gather_fusion
  33.2 0.9 fusion.25
  34.1 0.0 all-gather.6.cloned.1.call-update
  34.1 0.0 reduce-scatter.3.cloned.1.call-start
  34.2 32.8 %all-gather.6.cloned.1.call-done = bf16[160,4096]{1,0:T(8,128)(2,1)} async-done(((bf16[160,1024]{1,0:T(8,128)(2,1)}), bf16[160,4096]{1,0:T(8,128)(2,1)}) %all-gather.6.cloned.1.call-update) | async-done | bytes 1310736 | tf_op jit(solution)/shard_map/all_gather | solution.py:37
  66.9 5.3 %fusion.20 = bf16[160,1024]{1,0:T(8,128)(2,1)S(1)} fusion(bf16[160,4096]{1,0:T(8,128)(2,1)} %all-gather.6.cloned.1.call-done, bf16[4096,1024]{1,0:T(8,128)(2,1)} %param.14, f32[1024]{0:T(1024)S(1)} %add_divide_fusion.2), kind=kOutput, calls=%fused_computation.32 | convolution fusion | flops 1342504960 | bytes 10031104 | tf_op jit(solution)/shard_map/dot_general | solution.py:39
  72.3 7.8 %convolution_bitcast_fusion = f32[4096,160]{0,1:T(8,128)} fusion(bf16[160,1024]{1,0:T(8,128)(2,1)S(1)} %fusion.20, bf16[4096,1024]{1,0:T(8,128)(2,1)} %param.14), kind=kOutput, calls=%fused_computation.5 | convolution fusion | flops 1342177280 | bytes 11337728 | tf_op jit(solution)/shard_map/dot_general | solution.py:14
  80.1 0.0 reduce-scatter.3.cloned.1.call-update
  80.1 0.0 all-gather.8.cloned.1.call-start
  80.1 51.2 %reduce-scatter.3.cloned.1.call-done = f32[1024,160]{0,1:T(8,128)} async-done(((f32[4096,160]{0,1:T(8,128)}), f32[1024,160]{0,1:T(8,128)}) %reduce-scatter.3.cloned.1.call-update) | async-done | bytes 655376 | tf_op jit(solution)/shard_map/reduce_scatter | solution.py:41
  131.3 1.9 fusion.26
  133.3 0.2 all-reduce.2.cloned.1.call-start
  133.5 32.3 %all-gather.8.cloned.1.call-done = bf16[160,4096]{1,0:T(8,128)(2,1)} async-done(((bf16[160,1024]{1,0:T(8,128)(2,1)}), bf16[160,4096]{1,0:T(8,128)(2,1)}) %all-gather.8.cloned.1.call-update) | async-done | bytes 1310736 | tf_op jit(solution)/shard_map/all_gather | solution.py:45
  165.8 1.7 fusion.13
  167.5 16.2 %fusion.27 = f32[160,3584]{1,0:T(8,128)} fusion(bf16[4096,3584]{1,0:T(8,128)(2,1)} %param.17, bf16[160,4096]{1,0:T(8,128)(2,1)} %all-gather.8.cloned.1.call-done, f32[4096]{0:T(1024)S(1)} %convert_element_type.52, f32[160]{0:T(256)S(1)} %add_rsqrt_fusion), kind=kOutput, calls=%fused_computation.40 | convolution fusion | flops 4700241920 | bytes 32981632 | tf_op jit(solution)/shard_map/dot_general | solution.py:50
  183.7 25.1 %fusion.3 = f32[160,4096]{1,0:T(8,128)} fusion(bf16[4096,3584]{1,0:T(8,128)(2,1)} %param.17, bf16[4096,3584]{1,0:T(8,128)(2,1)} %param.18, bf16[160,3584]{1,0:T(8,128)(2,1)S(1)} %copy-done.6, f32[160,3584]{1,0:T(8,128)} %fusion.27, bf16[160,4096]{1,0:T(8,128)(2,1)S(1)} %copy-done, f32[4096]{0:T(1024)S(1)} %convert_element_type.52, f32[160]{0:T(256)S(1)} %add_rsqrt_fusion), kind=kOutput, calls=%fused_computation.11 | convolution fusion | flops 9404170240 | bytes 66110080 | tf_op jit(solution)/shard_map/dot_general | solution.py:14
  208.8 16.1 %convolution_add_fusion = f32[160,4096]{1,0:T(8,128)} fusion(f32[160,4096]{1,0:T(8,128)} %fusion.3, bf16[4096,3584]{1,0:T(8,128)(2,1)} %param.18, f32[160,3584]{1,0:T(8,128)} %fusion.27, bf16[160,3584]{1,0:T(8,128)(2,1)S(1)} %copy-done.6), kind=kOutput, calls=%fused_computation.6 | convolution fusion | flops 4702289920 | bytes 38043648 | tf_op jit(solution)/shard_map/dot_general | solution.py:14
  224.9 0.3 reduce-scatter.5.cloned.1.call-start
  225.2 103.0 %all-reduce.2.cloned.1.call-done = f32[160,4096]{1,0:T(8,128)} async-done(((f32[160,4096]{1,0:T(8,128)}), f32[160,4096]{1,0:T(8,128)}) %all-reduce.2.cloned.1.call-update) | async-done | bytes 2621456 | tf_op jit(solution)/shard_map/psum | solution.py:57
  328.2 2.3 fusion.14
  330.5 0.2 copy-done.1
  330.7 5.3 %fusion.21 = bf16[160,1024]{1,0:T(8,128)(2,1)S(1)} fusion(bf16[4096,1024]{1,0:T(8,128)(2,1)} %param.14, f32[1024]{0:T(1024)S(1)} %add_divide_fusion.2, bf16[160,4096]{1,0:T(8,128)(2,1)S(1)} %copy-done, f32[160,4096]{1,0:T(8,128)S(1)} %copy-done.1, f32[160]{0:T(256)S(1)} %fusion.14, f32[4096]{0:T(1024)S(1)} %convert_element_type.52, f32[160]{0:T(256)S(1)} %add_rsqrt_fusion), kind=kOutput, calls=%fused_computation.33 | convolution fusion | flops 1349058560 | bytes 12670208 | tf_op jit(solution)/shard_map/dot_general | solution.py:61
  336.1 8.3 %fusion.34 = f32[4096,1024]{1,0:T(8,128)} fusion(bf16[160,1024]{1,0:T(8,128)(2,1)S(1)} %fusion.20, bf16[160,4096]{1,0:T(8,128)(2,1)S(1)} %copy-done, f32[160,4096]{1,0:T(8,128)S(1)} %copy-done.1, f32[160]{0:T(256)S(1)} %fusion.14, f32[4096]{0:T(1024)S(1)} %convert_element_type.52, f32[160]{0:T(256)S(1)} %add_rsqrt_fusion), kind=kOutput, calls=%fused_computation.49 | convolution fusion | flops 1348730880 | bytes 21054720 | tf_op jit(solution)/shard_map/dot_general | solution.py:8
  344.4 11.4 %add_convert_fusion = bf16[4096,1024]{1,0:T(8,128)(2,1)} fusion(f32[4096,1024]{1,0:T(8,128)} %fusion.34, bf16[160,4096]{1,0:T(8,128)(2,1)S(1)} %copy-done.2, bf16[160,1024]{1,0:T(8,128)(2,1)S(1)} %fusion.21), kind=kOutput, calls=%fused_computation.1 | convolution fusion | flops 1350565888 | bytes 26804224 | tf_op jit(solution)/shard_map/dot_general | solution.py:8
  355.8 70.9 %reduce-scatter.5.cloned.1.call-done = bf16[1024,1024]{1,0:T(8,128)(2,1)} async-done(((bf16[4096,1024]{1,0:T(8,128)(2,1)}), bf16[1024,1024]{1,0:T(8,128)(2,1)}) %reduce-scatter.5.cloned.1.call-update) | async-done | bytes 2097168 | tf_op jit(solution)/shard_map/reduce_scatter | solution.py:64
  426.7 4.1 convert_element_type.60
  (20 shorter events, 0.1 us)
Async XLA Ops:
  7.2 26.0 %copy-start.3 = (bf16[160,1024]{1,0:T(8,128)(2,1)S(1)}, bf16[160,1024]{1,0:T(8,128)(2,1)}, u32[]{:S(2)}) copy-start(bf16[160,1024]{1,0:T(8,128)(2,1)} %param.10) | copy-start | bytes 983044
  7.2 27.0 %copy-start.5 = (f32[1024]{0:T(1024)S(1)}, f32[1024]{0:T(1024)}, u32[]{:S(2)}) copy-start(f32[1024]{0:T(1024)} %param.15) | copy-start | bytes 12292
  7.2 23.3 %all-gather.4.cloned.1.call-start = ((), (), s32[]{:S(2)}) async-start(), calls=%async_computation.2 | async-start | bytes 1638400 | tf_op jit(solution)/shard_map/all_gather | solution.py:34
  7.9 59.0 %all-gather.6.cloned.1.call-start = ((), (), s32[]{:S(2)}) async-start(), calls=%async_computation.3 | async-start | bytes 1638400 | tf_op jit(solution)/shard_map/all_gather | solution.py:37
  34.1 97.3 %reduce-scatter.3.cloned.1.call-start = ((), (), s32[]{:S(2)}) async-start(), calls=%async_computation.4 | async-start | bytes 3276800 | tf_op jit(solution)/shard_map/reduce_scatter | solution.py:41
  80.1 53.4 %copy-start.4 = (bf16[4096]{0:T(1024)(128)(2,1)S(1)}, bf16[4096]{0:T(1024)(128)(2,1)}, u32[]{:S(2)}) copy-start(bf16[4096]{0:T(1024)(128)(2,1)} %param.16) | copy-start | bytes 24580
  80.1 85.7 %all-gather.8.cloned.1.call-start = ((), (), s32[]{:S(2)}) async-start(), calls=%async_computation.5 | async-start | bytes 1638400 | tf_op jit(solution)/shard_map/all_gather | solution.py:45
  133.3 194.9 %all-reduce.2.cloned.1.call-start = ((), (), s32[]{:S(2)}) async-start(), calls=%async_computation.6 | async-start | bytes 5242880 | tf_op jit(solution)/shard_map/psum | solution.py:57
  167.5 16.2 %copy-start = (bf16[160,4096]{1,0:T(8,128)(2,1)S(1)}, bf16[160,4096]{1,0:T(8,128)(2,1)}, u32[]{:S(2)}) copy-start(bf16[160,4096]{1,0:T(8,128)(2,1)} %all-gather.8.cloned.1.call-done) | copy-start | bytes 3932164
  167.5 16.2 %copy-start.6 = (bf16[160,3584]{1,0:T(8,128)(2,1)S(1)}, bf16[160,3584]{1,0:T(8,128)(2,1)}, u32[]{:S(2)}) copy-start(bf16[160,3584]{1,0:T(8,128)(2,1)} %param.19) | copy-start | bytes 3440644
  224.9 201.8 %reduce-scatter.5.cloned.1.call-start = ((), (), s32[]{:S(2)}) async-start(), calls=%async_computation.7 | async-start | bytes 10485760 | tf_op jit(solution)/shard_map/reduce_scatter | solution.py:64
  328.2 2.5 copy-start.1
  336.0 8.4 %copy-start.2 = (bf16[160,4096]{1,0:T(8,128)(2,1)S(1)}, bf16[160,4096]{1,0:T(8,128)(2,1)}, u32[]{:S(2)}) copy-start(bf16[160,4096]{1,0:T(8,128)(2,1)} %all-gather.6.cloned.1.call-done) | copy-start | bytes 3932164
Sparse Core Ops, SparseCore 0:
  9.6 20.8 all-gather.3
  34.2 32.6 all-gather.5
  80.2 51.0 reduce-scatter.2
  133.4 32.3 all-gather.7
  225.0 103.0 all-reduce.1
  355.9 70.7 reduce-scatter.4
where the time goes:
time: 438 us
  waiting for transfers between devices  312 us (71%)
  matrix products  95.6 us (22%)
  between operations  14.2 us (3%)
  other arithmetic  12.2 us (3%)
    psum x1, waiting for transfers between devices, shards(): dnormed = lax.psum(partial_grad, 'mp')  103 us
    reduce_scatter x1, waiting for transfers between devices, shards(): lax.psum_scatter((contract_first(dinter, weighted) + contract_first(diff_...  70.9 us
    reduce_scatter x1, waiting for transfers between devices, shards(): lax.psum_scatter(contract_last(rotation, weighted), 'mp', scatter_dimensi...  51.2 us
    dot_general x3, matrix products, contract_last(): lax.dot_general(left, right, (((1,), (1,)), ((), ())), preferred_element_...  49 us
    all_gather x1, waiting for transfers between devices, shards(): diff_full = lax.all_gather(diff_local, 'mp', axis=1, tiled=True)  32.8 us
    all_gather x1, waiting for transfers between devices, shards(): full_rows = lax.all_gather(interchanged, 'mp', axis=1, tiled=True)  32.3 us
    all_gather x1, waiting for transfers between devices, shards(): everyone = lax.all_gather(source_states, 'dp', axis=0, tiled=True)  21.2 us
    dot_general x2, matrix products, contract_first(): lax.dot_general(left, right, (((0,), (0,)), ((), ())), preferred_element_...  19.7 us
  transfers between devices with their start and end apart: 6, of which 6 were waited for; matrix products, arithmetic and copies ran while one was open for 0% of the time, Pallas kernels for 0%

commit v1 on v0

--- a/solution.py
+++ b/solution.py
@@ -42,7 +42,14 @@
         contract_last(rotation, weighted), "mp", scatter_dimension=0, tiled=True
     ).T
     interchanged = (base_states.astype(jnp.float32) + moved).astype(jnp.bfloat16)
-    full_rows = lax.all_gather(interchanged, "mp", axis=1, tiled=True)
+    ways = lax.axis_size("mp")
+    pieces = [interchanged]
+    for far in range(1, ways):
+        pieces.append(
+            lax.ppermute(pieces[far - 1], "mp", [(d, (d - 1) % ways) for d in range(ways)])
+        )
+    line = jnp.concatenate(pieces, axis=1)
+    full_rows = jnp.roll(line, lax.axis_index("mp") * interchanged.shape[1], axis=1)
     states = full_rows.astype(jnp.float32)
     gain_f = norm_gain.astype(jnp.float32)[None, :]
     recip = lax.rsqrt(jnp.mean(states * states, axis=1, keepdims=True) + 1e-05)

time: 438 us -> 437 us (level)
  waiting for transfers between devices: 312 us -> 302 us
  starting transfers between devices: 0.64 us -> 10.4 us
    all_gather x1 -> x0, waiting for transfers between devices: 32.3 us -> none  [shards(): full_rows = lax.all_gather(interchanged, 'mp', axis=1, tiled=True)]
    ppermute x0 -> x3, waiting for transfers between devices: none -> 19.3 us  [shards(): lax.ppermute(pieces[far - 1], 'mp', [(d, (d - 1) % ways) for d in range(w...]
    ppermute x0 -> x3, starting transfers between devices: none -> 10 us  [shards(): lax.ppermute(pieces[far - 1], 'mp', [(d, (d - 1) % ways) for d in range(w...]
  transfers between devices with their start and end apart: 6 -> 8, of which waited for: 6 -> 8; matrix products, arithmetic and copies ran while one was open for 0% -> 0% of each run, Pallas kernels for 0% -> 0%
where the time goes in v1:
time: 437 us; the launch traced here: 436 us
  waiting for transfers between devices  302 us (69%)
  matrix products  93.4 us (21%)
  between operations  13.9 us (3%)
  starting transfers between devices  10.4 us (2%)
  other arithmetic  10.2 us (2%)
  local copies, waits for them, and re-layouts  6.71 us (2%)
    psum x1, waiting for transfers between devices, shards(): dnormed = lax.psum(partial_grad, 'mp')  106 us
    reduce_scatter x1, waiting for transfers between devices, shards(): lax.psum_scatter((contract_first(dinter, weighted) + contract_first(diff_...  70.9 us
    reduce_scatter x1, waiting for transfers between devices, shards(): lax.psum_scatter(contract_last(rotation, weighted), 'mp', scatter_dimensi...  51.2 us
    dot_general x3, matrix products, contract_last(): lax.dot_general(left, right, (((1,), (1,)), ((), ())), preferred_element_...  49.6 us
    all_gather x1, waiting for transfers between devices, shards(): diff_full = lax.all_gather(diff_local, 'mp', axis=1, tiled=True)  32.8 us
    all_gather x1, waiting for transfers between devices, shards(): everyone = lax.all_gather(source_states, 'dp', axis=0, tiled=True)  21.2 us
    dot_general x2, matrix products, contract_first(): lax.dot_general(left, right, (((0,), (0,)), ((), ())), preferred_element_...  19.7 us
    ppermute x3, waiting for transfers between devices, shards(): lax.ppermute(pieces[far - 1], 'mp', [(d, (d - 1) % ways) for d in range(w...  19.3 us
  transfers between devices with their start and end apart: 8, of which 8 were waited for; matrix products, arithmetic and copies ran while one was open for 0% of the time, Pallas kernels for 0%

profile of v1, /device:TPU:0, one launch (start us, length us, event | category | flops | bytes accessed | tf_op | source)
XLA Modules:
  0.0 436.4 jit_solution(10099674698618140222)
XLA Ops:
  7.2 0.7 all-gather.3.cloned.1.call-update
  8.0 0.7 broadcast_multiply_fusion
  8.6 0.7 compare_and_fusion
  9.3 21.2 %all-gather.3.cloned.1.call-done = bf16[640,1024]{1,0:T(8,128)(2,1)} async-done(((bf16[160,1024]{1,0:T(8,128)(2,1)}), bf16[640,1024]{1,0:T(8,128)(2,1)}) %all-gather.3.cloned.1.call-update) | async-done | bytes 1310736 | tf_op jit(solution)/shard_map/all_gather | solution.py:34
  30.5 2.7 gather_fusion
  33.2 0.9 fusion.25
  34.2 32.8 %all-gather.5.cloned.1.call-done = bf16[160,4096]{1,0:T(8,128)(2,1)} async-done(((bf16[160,1024]{1,0:T(8,128)(2,1)}), bf16[160,4096]{1,0:T(8,128)(2,1)}) %all-gather.5.cloned.1.call-update) | async-done | bytes 1310736 | tf_op jit(solution)/shard_map/all_gather | solution.py:37
  66.9 5.3 %fusion.20 = bf16[160,1024]{1,0:T(8,128)(2,1)S(1)} fusion(bf16[160,4096]{1,0:T(8,128)(2,1)} %all-gather.5.cloned.1.call-done, bf16[4096,1024]{1,0:T(8,128)(2,1)} %param.14, f32[1024]{0:T(1024)S(1)} %add_divide_fusion.2), kind=kOutput, calls=%fused_computation.32 | convolution fusion | flops 1342504960 | bytes 10031104 | tf_op jit(solution)/shard_map/dot_general | solution.py:39
  72.3 0.7 copy-done.4
  73.0 7.8 %convolution_bitcast_fusion = f32[4096,160]{0,1:T(8,128)} fusion(bf16[160,1024]{1,0:T(8,128)(2,1)S(1)} %fusion.20, bf16[4096,1024]{1,0:T(8,128)(2,1)} %param.14), kind=kOutput, calls=%fused_computation.5 | convolution fusion | flops 1342177280 | bytes 11337728 | tf_op jit(solution)/shard_map/dot_general | solution.py:14
  80.9 51.2 %reduce-scatter.3.cloned.1.call-done = f32[1024,160]{0,1:T(8,128)} async-done(((f32[4096,160]{0,1:T(8,128)}), f32[1024,160]{0,1:T(8,128)}) %reduce-scatter.3.cloned.1.call-update) | async-done | bytes 655376 | tf_op jit(solution)/shard_map/reduce_scatter | solution.py:41
  132.1 1.2 constant_dynamic-update-slice_fusion.7
  133.3 1.8 collective-permute-start
  135.1 7.5 %collective-permute-done = bf16[160,1024]{1,0:T(8,128)(2,1)S(1)} collective-permute-done((bf16[160,1024]{1,0:T(8,128)(2,1)S(1)}, bf16[160,1024]{1,0:T(8,128)(2,1)S(1)}, u32[]{:S(2)}, u32[]{:S(2)}) %collective-permute-start) | collective-permute-done | bytes 327712 | tf_op jit(solution)/shard_map/ppermute | solution.py:49
  142.7 3.9 collective-permute-start.1
  146.6 6.3 %collective-permute-done.1 = bf16[160,1024]{1,0:T(8,128)(2,1)S(1)} collective-permute-done((bf16[160,1024]{1,0:T(8,128)(2,1)S(1)}, bf16[160,1024]{1,0:T(8,128)(2,1)S(1)}, u32[]{:S(2)}, u32[]{:S(2)}) %collective-permute-start.1) | collective-permute-done | bytes 327712 | tf_op jit(solution)/shard_map/ppermute | solution.py:49
  152.9 4.3 collective-permute-start.2
  157.3 5.4 %collective-permute-done.2 = bf16[160,1024]{1,0:T(8,128)(2,1)} collective-permute-done((bf16[160,1024]{1,0:T(8,128)(2,1)S(1)}, bf16[160,1024]{1,0:T(8,128)(2,1)}, u32[]{:S(2)}, u32[]{:S(2)}) %collective-permute-start.2) | collective-permute-done | bytes 327712 | tf_op jit(solution)/shard_map/ppermute | solution.py:49
  162.6 1.0 constant_dynamic-update-slice_fusion.4
  163.6 1.0 constant_dynamic-update-slice_fusion.3
  164.7 1.0 constant_dynamic-update-slice_fusion
  165.7 0.4 fusion.13
  166.1 13.4 %fusion.27 = f32[160,3584]{1,0:T(8,128)} fusion(bf16[4096,3584]{1,0:T(8,128)(2,1)} %param.17, f32[4096]{0:T(1024)S(1)} %convert_element_type.52, f32[160]{0:T(256)S(1)} %add_rsqrt_fusion, bf16[160,8192]{1,0:T(8,128)(2,1)S(1)} %constant_dynamic-update-slice_fusion, s32[]{:T(128)S(6)} %select_n.25), kind=kOutput, calls=%fused_computation.40 | convolution fusion | flops 4700241920 | bytes 32982020 | tf_op jit(solution)/shard_map/dot_general | solution.py:57
  179.4 25.4 %fusion.3 = f32[160,4096]{1,0:T(8,128)} fusion(bf16[4096,3584]{1,0:T(8,128)(2,1)} %param.17, bf16[4096,3584]{1,0:T(8,128)(2,1)} %param.18, bf16[160,3584]{1,0:T(8,128)(2,1)} %param.19, f32[160,3584]{1,0:T(8,128)} %fusion.27, f32[4096]{0:T(1024)S(1)} %convert_element_type.52, f32[160]{0:T(256)S(1)} %add_rsqrt_fusion, ...), kind=kOutput, calls=%fused_computation.11 | convolution fusion | flops 9404170240 | bytes 66110468 | tf_op jit(solution)/shard_map/dot_general | solution.py:14
  204.8 16.4 %convolution_add_fusion = f32[160,4096]{1,0:T(8,128)} fusion(f32[160,4096]{1,0:T(8,128)} %fusion.3, bf16[4096,3584]{1,0:T(8,128)(2,1)} %param.18, f32[160,3584]{1,0:T(8,128)} %fusion.27, bf16[160,3584]{1,0:T(8,128)(2,1)} %param.19), kind=kOutput, calls=%fused_computation.6 | convolution fusion | flops 4702289920 | bytes 38043648 | tf_op jit(solution)/shard_map/dot_general | solution.py:14
  221.5 105.7 %all-reduce.2.cloned.1.call-done = f32[160,4096]{1,0:T(8,128)} async-done(((f32[160,4096]{1,0:T(8,128)}), f32[160,4096]{1,0:T(8,128)}) %all-reduce.2.cloned.1.call-update) | async-done | bytes 2621456 | tf_op jit(solution)/shard_map/psum | solution.py:64
  327.2 2.3 fusion.14
  329.8 5.4 %fusion.21 = bf16[160,1024]{1,0:T(8,128)(2,1)S(1)} fusion(bf16[4096,1024]{1,0:T(8,128)(2,1)} %param.14, f32[1024]{0:T(1024)S(1)} %add_divide_fusion.2, f32[160,4096]{1,0:T(8,128)S(1)} %copy-done, f32[160]{0:T(256)S(1)} %fusion.14, f32[4096]{0:T(1024)S(1)} %convert_element_type.52, f32[160]{0:T(256)S(1)} %add_rsqrt_fusion, ...), kind=kOutput, calls=%fused_computation.33 | convolution fusion | flops 1349058560 | bytes 12670980 | tf_op jit(solution)/shard_map/dot_general | solution.py:68
  335.2 8.3 %fusion.38 = f32[4096,1024]{1,0:T(8,128)} fusion(bf16[160,1024]{1,0:T(8,128)(2,1)S(1)} %copy-done.5, f32[160,4096]{1,0:T(8,128)S(1)} %copy-done, f32[160]{0:T(256)S(1)} %fusion.14, f32[4096]{0:T(1024)S(1)} %convert_element_type.52, f32[160]{0:T(256)S(1)} %add_rsqrt_fusion, bf16[160,8192]{1,0:T(8,128)(2,1)S(1)} %constant_dynamic-update-slice_fusion, ...), kind=kOutput, calls=%fused_computation.59 | convolution fusion | flops 1348730880 | bytes 21055492 | tf_op jit(solution)/shard_map/dot_general | solution.py:8
  343.5 11.4 %add_convert_fusion = bf16[4096,1024]{1,0:T(8,128)(2,1)} fusion(f32[4096,1024]{1,0:T(8,128)} %fusion.38, bf16[160,4096]{1,0:T(8,128)(2,1)S(1)} %copy-done.1, bf16[160,1024]{1,0:T(8,128)(2,1)S(1)} %fusion.21), kind=kOutput, calls=%fused_computation.1 | convolution fusion | flops 1350565888 | bytes 26804224 | tf_op jit(solution)/shard_map/dot_general | solution.py:8
  354.9 70.9 %reduce-scatter.5.cloned.1.call-done = bf16[1024,1024]{1,0:T(8,128)(2,1)} async-done(((bf16[4096,1024]{1,0:T(8,128)(2,1)}), bf16[1024,1024]{1,0:T(8,128)(2,1)}) %reduce-scatter.5.cloned.1.call-update) | async-done | bytes 2097168 | tf_op jit(solution)/shard_map/reduce_scatter | solution.py:71
  425.8 4.1 convert_element_type.60
  (32 shorter events, 0.8 us)
Async XLA Ops:
  7.2 26.0 %copy-start.2 = (bf16[160,1024]{1,0:T(8,128)(2,1)S(1)}, bf16[160,1024]{1,0:T(8,128)(2,1)}, u32[]{:S(2)}) copy-start(bf16[160,1024]{1,0:T(8,128)(2,1)} %param.10) | copy-start | bytes 983044
  7.2 27.0 %copy-start.7 = (f32[1024]{0:T(1024)S(1)}, f32[1024]{0:T(1024)}, u32[]{:S(2)}) copy-start(f32[1024]{0:T(1024)} %param.15) | copy-start | bytes 12292
  7.2 23.3 %all-gather.3.cloned.1.call-start = ((), (), s32[]{:S(2)}) async-start(), calls=%async_computation.2 | async-start | bytes 1638400 | tf_op jit(solution)/shard_map/all_gather | solution.py:34
  7.9 59.0 %all-gather.5.cloned.1.call-start = ((), (), s32[]{:S(2)}) async-start(), calls=%async_computation.3 | async-start | bytes 1638400 | tf_op jit(solution)/shard_map/all_gather | solution.py:37
  34.1 98.0 %reduce-scatter.3.cloned.1.call-start = ((), (), s32[]{:S(2)}) async-start(), calls=%async_computation.4 | async-start | bytes 3276800 | tf_op jit(solution)/shard_map/reduce_scatter | solution.py:41
  72.3 0.7 copy-start.4
  80.8 76.4 %copy-start.6 = (bf16[4096]{0:T(1024)(128)(2,1)S(1)}, bf16[4096]{0:T(1024)(128)(2,1)}, u32[]{:S(2)}) copy-start(bf16[4096]{0:T(1024)(128)(2,1)} %param.16) | copy-start | bytes 24580
  80.9 246.4 %all-reduce.2.cloned.1.call-start = ((), (), s32[]{:S(2)}) async-start(), calls=%async_computation.5 | async-start | bytes 5242880 | tf_op jit(solution)/shard_map/psum | solution.py:64
  133.3 19.6 %copy-start.3 = (bf16[160,1024]{1,0:T(8,128)(2,1)}, bf16[160,1024]{1,0:T(8,128)(2,1)S(1)}, u32[]{:S(2)}) copy-start(bf16[160,1024]{1,0:T(8,128)(2,1)S(1)} %get-tuple-element.3) | copy-start | bytes 983044
  133.3 9.3 %collective-permute-start = (bf16[160,1024]{1,0:T(8,128)(2,1)S(1)}, bf16[160,1024]{1,0:T(8,128)(2,1)S(1)}, u32[]{:S(2)}, u32[]{:S(2)}) collective-permute-start(bf16[160,1024]{1,0:T(8,128)(2,1)S(1)} %get-tuple-element.3), channel_id=1, source_target_pairs={{0,3},{1,0},{2,1},{3,2},{4,7},{5,4},{6,5},{7,6},{8,11},{9,8},{10,9... | collective-permute-start | bytes 983048 | tf_op jit(solution)/shard_map/ppermute | solution.py:49
  142.7 10.3 %collective-permute-start.1 = (bf16[160,1024]{1,0:T(8,128)(2,1)S(1)}, bf16[160,1024]{1,0:T(8,128)(2,1)S(1)}, u32[]{:S(2)}, u32[]{:S(2)}) collective-permute-start(bf16[160,1024]{1,0:T(8,128)(2,1)S(1)} %collective-permute-done), channel_id=1, source_target_pairs={{0,3},{1,0},{2,1},{3,2},{4,7},{5,4},{6,5},{7,6},{8,11},{9,8},{10,9... | collective-permute-start | bytes 983048 | tf_op jit(solution)/shard_map/ppermute | solution.py:49
  152.9 9.7 %collective-permute-start.2 = (bf16[160,1024]{1,0:T(8,128)(2,1)S(1)}, bf16[160,1024]{1,0:T(8,128)(2,1)}, u32[]{:S(2)}, u32[]{:S(2)}) collective-permute-start(bf16[160,1024]{1,0:T(8,128)(2,1)S(1)} %collective-permute-done.1), channel_id=1, source_target_pairs={{0,3},{1,0},{2,1},{3,2},{4,7},{5,4},{6,5},{7,6},{8,11},{9,8},{10,9... | collective-permute-start | bytes 983048 | tf_op jit(solution)/shard_map/ppermute | solution.py:49
  221.3 204.5 %reduce-scatter.5.cloned.1.call-start = ((), (), s32[]{:S(2)}) async-start(), calls=%async_computation.6 | async-start | bytes 10485760 | tf_op jit(solution)/shard_map/reduce_scatter | solution.py:71
  327.2 2.5 copy-start
  329.8 5.4 %copy-start.5 = (bf16[160,1024]{1,0:T(8,128)(2,1)S(1)}, bf16[160,1024]{1,0:T(8,128)(2,1)}, u32[]{:S(2)}) copy-start(bf16[160,1024]{1,0:T(8,128)(2,1)} %copy-done.4) | copy-start | bytes 983044
  335.2 8.3 %copy-start.1 = (bf16[160,4096]{1,0:T(8,128)(2,1)S(1)}, bf16[160,4096]{1,0:T(8,128)(2,1)}, u32[]{:S(2)}) copy-start(bf16[160,4096]{1,0:T(8,128)(2,1)} %all-gather.5.cloned.1.call-done) | copy-start | bytes 3932164
Sparse Core Ops, SparseCore 0:
  9.6 20.8 all-gather.2
  34.2 32.6 all-gather.4
  81.0 51.0 reduce-scatter.2
  221.4 105.7 all-reduce.1
  355.0 70.7 reduce-scatter.4
